TPU v7x, 32 devices: a whole 2x2x4 slice. The times are simulated.
32 devices in a mesh: dp: 4 (over z), ctx: 2 (over core), tp: 4 (over y, x).
Axes of the slice: x: 2, y: 2, z: 4, core: 2. Of those that a mesh axis runs over, the one named last changes fastest.
Arguments:
- block_in: bfloat16 [8192, 2048], P(('dp', 'ctx')), may hold values from -6 to 6
- query_proj: bfloat16 [2048, 2048], P('dp', 'tp'), may hold values from -0.125 to 0.125
- forget_proj: bfloat16 [2048, 2048], P('dp', 'tp'), may hold values from -0.0625 to 0.0625
- value_proj: bfloat16 [2048, 2048], P('dp', 'tp'), may hold values from -0.125 to 0.125
- outgate_proj: bfloat16 [2048, 2048], P('dp', 'tp'), may hold values from -0.125 to 0.125
- out_proj: bfloat16 [2048, 2048], P('tp', 'dp'), may hold values from -0.125 to 0.125
- ffn_gate: bfloat16 [2048, 5632], P('dp', 'tp'), may hold values from -0.125 to 0.125
- ffn_up: bfloat16 [2048, 5632], P('dp', 'tp'), may hold values from -0.125 to 0.125
- ffn_down: bfloat16 [5632, 2048], P('tp', 'dp'), may hold values from -0.078125 to 0.078125
- first_gain: float32 [2048], replicated, may hold values from 0.5 to 1.5
- second_gain: float32 [2048], replicated, may hold values from 0.5 to 1.5
- group_gain: float32 [2048], P('tp'), may hold values from 0.5 to 1.5
- forget_bias: float32 [2048], P('tp'), may hold values from 3 to 12
- bound_table: float32 [24, 2048], P(None, 'tp'), may hold values from -4 to 4
- layer_index: int32 [1], replicated, may hold values from 1 to 23
- second_start: int32 [4], P('dp'), may hold values from 1 to 2048, as said below
- cotangent: bfloat16 [8192, 2048], P(('dp', 'ctx')), may hold values from -6 to 6
Outputs:
- block_out: bfloat16 [8192, 2048], P(('dp', 'ctx'))
- input_grad: float32 [8192, 2048], P(('dp', 'ctx'))
- query_grad: float32 [2048, 2048], P('dp', 'tp')
- forget_grad: float32 [2048, 2048], P('dp', 'tp')
- value_grad: float32 [2048, 2048], P('dp', 'tp')
- outgate_grad: float32 [2048, 2048], P('dp', 'tp')
- out_proj_grad: float32 [2048, 2048], P('tp', 'dp')
- ffn_gate_grad: float32 [2048, 5632], P('dp', 'tp')
- ffn_up_grad: float32 [2048, 5632], P('dp', 'tp')
- ffn_down_grad: float32 [5632, 2048], P('tp', 'dp')
- first_gain_grad: float32 [2048], replicated
- second_gain_grad: float32 [2048], replicated
- group_gain_grad: float32 [2048], P('tp')
- forget_bias_grad: float32 [2048], P('tp')
- bound_table_grad: float32 [24, 2048], P(None, 'tp')
Inputs may be any that keep to these rules, and one draw needn't show every extreme that they name: second_start[p] is 2048 where pack p is one whole sequence, and otherwise the position inside the pack where its second sequence begins; pack 0 is always one whole sequence and pack 1 always holds two. layer_index names a row of bound_table other than the first.
All inputs are finite; a program needn't handle non-finite values.
Results may differ from a plain program's by a relative error of at most 0.018.
Values may be sent and summed in bfloat16 or wider, within the bound.
No kernel may reach another device: no remote copies, remote signals or barrier semaphores. Data moves between devices by JAX's collectives and lax.ppermute only.
A program may use at most 384 MiB of HBM per device.

v0:
```python
import jax
import jax.numpy as jnp
from jax import lax
from jax.sharding import PartitionSpec as P

HEAD = 128
BLOCK = 32
HIGH = lax.Precision.HIGHEST
EPS_NORM = 1e-06
EPS_GROUP = 1e-05


def carried_in(value, axis, join, neutral):
    count, mine = (lax.axis_size(axis), lax.axis_index(axis))
    pieces = jax.tree.map(lambda part: lax.all_gather(part, axis), value)
    total = jax.tree.map(
        lambda part, zero: jnp.full_like(part, 0) + jnp.asarray(zero, part.dtype), value, neutral
    )

    def hop(position, total):
        longer = join(total, jax.tree.map(lambda part: part[position], pieces))
        return jax.tree.map(lambda new, old: jnp.where(position < mine, new, old), longer, total)

    return lax.fori_loop(0, count - 1, hop, total)


def carried_in_2(array, axis, combine, identity):
    peers, index = (lax.axis_size(axis), lax.axis_index(axis))
    everything = jax.tree.map(
        lambda part, kind: lax.all_gather(part.astype(kind), axis),
        array,
        jax.tree.map(lambda a: jnp.bfloat16 if a.dtype == jnp.float32 else a.dtype, array),
    )
    start = jax.tree.map(
        lambda part, zero: jnp.broadcast_to(jnp.asarray(zero, part.dtype), part.shape),
        array,
        identity,
    )

    def hop(k, before):
        at = peers - 1 - k
        reached = at > index
        new = combine(
            before, jax.tree.map(lambda part, own: part[at].astype(own.dtype), everything, array)
        )
        return jax.tree.map(lambda a, b: jnp.where(reached, a, b), new, before)

    return lax.fori_loop(0, peers, hop, start)


def rms_norm(rows_in, gain_vec):
    return (
        rows_in
        * lax.rsqrt(jnp.mean(rows_in * rows_in, axis=-1, keepdims=True) + EPS_NORM)
        * gain_vec
    )


def head_norm(mixed, pre_gate, gain_vec, head_count):
    row_count = mixed.shape[0]
    grouped = mixed.reshape(row_count, head_count, -1)
    scaled = grouped * lax.rsqrt(jnp.mean(grouped * grouped, axis=-1, keepdims=True) + EPS_GROUP)
    return scaled.reshape(row_count, -1) * gain_vec * jax.nn.silu(pre_gate)


def lower_bound(bound_rows, which_layer):
    weights = jax.nn.softmax(bound_rows, axis=0)
    rising = jnp.cumsum(weights, axis=0) - weights[0:1]
    picked = (
        lax.broadcasted_iota(jnp.int32, (bound_rows.shape[0], 1), 0) == which_layer[0]
    ).astype(bound_rows.dtype)
    return jnp.sum(rising * picked, axis=0)


def gate_values(pre_query, pre_forget, bias_vec, bound_vec):
    shifted = pre_forget + bias_vec
    forget = bound_vec + (1.0 - bound_vec) * jax.nn.sigmoid(shifted)
    return (jax.nn.silu(pre_query), (1.0 - bound_vec) * jax.nn.sigmoid(-shifted), jnp.log(forget))


def chain_link(earlier, later):
    return (earlier[0] * later[0], later[0][..., None] * earlier[1] + later[1])


def contract_last(left_side, right_side):
    return lax.dot_general(
        left_side, right_side, (((1,), (1,)), ((), ())), preferred_element_type=jnp.float32
    )


def contract_first(left_side, right_side):
    return lax.dot_general(
        left_side, right_side, (((0,), (0,)), ((), ())), preferred_element_type=jnp.float32
    )


def block_parts(queries, key_rows, values, log_forget, doc_ids, prev_doc, block_len):
    length, head_count, feature = queries.shape
    block_count = length // block_len
    blocked = (block_count, block_len, head_count, feature)
    queries = queries.reshape(blocked)
    key_rows = key_rows.reshape(blocked)
    values = values.reshape(blocked)
    decays = jnp.cumsum(log_forget.reshape(blocked), axis=1)
    doc_ids = doc_ids.reshape(block_count, block_len)
    before = jnp.concatenate([jnp.reshape(prev_doc, (1,)), doc_ids[:-1, block_len - 1]])
    middle = decays[:, block_len // 2 : block_len // 2 + 1]
    final_decay = decays[:, block_len - 1 :]
    scores = jnp.einsum(
        "nthc,nshc->nhts",
        queries * jnp.exp(decays - middle),
        key_rows * jnp.exp(middle - decays),
        precision=HIGH,
    )
    causal = lax.broadcasted_iota(jnp.int32, (block_len, block_len), 0) >= lax.broadcasted_iota(
        jnp.int32, (block_len, block_len), 1
    )
    allowed = causal[None] & (doc_ids[:, :, None] == doc_ids[:, None, :])
    scores = jnp.where(allowed[:, None], scores, 0.0)
    inside = jnp.einsum("nhts,nshe->nthe", scores, values, precision=HIGH)
    in_tail = (doc_ids == doc_ids[:, block_len - 1 :]).astype(decays.dtype)
    ending = key_rows * jnp.exp(final_decay - decays) * in_tail[:, :, None, None]
    states = jnp.einsum("nshc,nshe->nhce", ending, values, precision=HIGH)
    kept_flag = (doc_ids[:, block_len - 1] == before).astype(decays.dtype)
    carried = jnp.exp(final_decay[:, 0]) * kept_flag[:, None, None]
    entering = (doc_ids == before[:, None]).astype(decays.dtype)
    reached = queries * jnp.exp(decays) * entering[:, :, None, None]
    prefix_decay, prefix_state = lax.associative_scan(chain_link, (carried, states), axis=0)
    return (inside, reached, prefix_decay, prefix_state)


def finish(pieces, state_in):
    inside, reached, prefix_decay, prefix_state = pieces
    state_ends = prefix_decay[..., None] * state_in[None] + prefix_state
    state_starts = jnp.concatenate([state_in[None], state_ends[:-1]], axis=0)
    outside = jnp.einsum("nthc,nhce->nthe", reached, state_starts, precision=HIGH)
    summed = inside + outside
    block_count, block_len, head_count, feature = summed.shape
    return (summed.reshape(block_count * block_len, head_count, feature), state_ends[-1])


def body(
    block_in,
    query_proj,
    forget_proj,
    value_proj,
    outgate_proj,
    out_proj,
    ffn_gate,
    ffn_up,
    ffn_down,
    first_gain,
    second_gain,
    group_gain,
    forget_bias,
    bound_table,
    layer_index,
    second_start,
    cotangent,
):
    row_count = block_in.shape[0]
    local_width = query_proj.shape[1]
    head_count = local_width // HEAD
    hidden_width = ffn_gate.shape[1]
    inputs = block_in.astype(jnp.float32)
    first_low = rms_norm(inputs, first_gain).astype(jnp.bfloat16)
    mix_local = jnp.concatenate([query_proj, forget_proj, value_proj, outgate_proj], axis=1)
    ffn_local = jnp.concatenate([ffn_gate, ffn_up], axis=1)
    mix_full, out_full = (
        lax.all_gather(mix_local, "dp", axis=0, tiled=True),
        lax.all_gather(out_proj, "dp", axis=1, tiled=True),
    )
    projected = jnp.dot(first_low, mix_full, preferred_element_type=jnp.float32)
    pre_query = projected[:, :local_width]
    pre_forget = projected[:, local_width : 2 * local_width]
    pre_value = projected[:, 2 * local_width : 3 * local_width]
    pre_outgate = projected[:, 3 * local_width :]
    bound_vec = lower_bound(bound_table, layer_index)
    queries, key_rows, log_forget = gate_values(pre_query, pre_forget, forget_bias, bound_vec)
    offset = lax.axis_index("ctx") * row_count
    doc_ids = (offset + lax.iota(jnp.int32, row_count) >= second_start[0]).astype(jnp.int32)
    prev_doc = (offset - 1 >= second_start[0]).astype(jnp.int32)

    def to_heads(flat):
        return flat.reshape(row_count, head_count, HEAD)

    def mixer(queries_in, keys_in, values_in, logs_in, state_in):
        return finish(
            block_parts(queries_in, keys_in, values_in, logs_in, doc_ids, prev_doc, BLOCK), state_in
        )

    pieces = block_parts(
        to_heads(queries),
        to_heads(key_rows),
        to_heads(pre_value),
        to_heads(log_forget),
        doc_ids,
        prev_doc,
        BLOCK,
    )
    identity = (
        jnp.ones((head_count, HEAD), jnp.float32),
        jnp.zeros((head_count, HEAD, HEAD), jnp.float32),
    )
    shard_decay = pieces[2][-1]
    entry_pair = carried_in((shard_decay, pieces[3][-1]), "ctx", chain_link, identity)
    state_in = entry_pair[1]
    mixed, _ = finish(pieces, state_in)
    mixed_flat = mixed.reshape(row_count, local_width)
    gated_low = head_norm(mixed_flat, pre_outgate, group_gain, head_count).astype(jnp.bfloat16)
    mix_partial = jnp.dot(gated_low, out_full, preferred_element_type=jnp.float32)
    resid = inputs + lax.psum(mix_partial, "tp")
    second_low = rms_norm(resid, second_gain).astype(jnp.bfloat16)
    ffn_full, down_full = (
        lax.all_gather(ffn_local, "dp", axis=0, tiled=True),
        lax.all_gather(ffn_down, "dp", axis=1, tiled=True),
    )
    gate_up = jnp.dot(second_low, ffn_full, preferred_element_type=jnp.float32)
    pre_gate = gate_up[:, :hidden_width]
    pre_up = gate_up[:, hidden_width:]
    hidden_low = (jax.nn.silu(pre_gate) * pre_up).astype(jnp.bfloat16)
    ffn_partial = jnp.dot(hidden_low, down_full, preferred_element_type=jnp.float32)
    block_out = (
        resid + lax.psum(ffn_partial.astype(jnp.bfloat16), "tp").astype(jnp.float32)
    ).astype(jnp.bfloat16)
    mix_full, out_full, ffn_full, down_full = (
        lax.all_gather(mix_local, "dp", axis=0, tiled=True),
        lax.all_gather(out_proj, "dp", axis=1, tiled=True),
        lax.all_gather(ffn_local, "dp", axis=0, tiled=True),
        lax.all_gather(ffn_down, "dp", axis=1, tiled=True),
    )
    cotangent_full = cotangent.astype(jnp.float32)
    hidden_grad = contract_last(cotangent, down_full)
    down_weight_grad = contract_first(hidden_low, cotangent)
    _, act_pull = jax.vjp(lambda gate_in, up_in: jax.nn.silu(gate_in) * up_in, pre_gate, pre_up)
    gate_grad, up_grad = act_pull(hidden_grad)
    gate_up_grad = jnp.concatenate([gate_grad, up_grad], axis=1).astype(jnp.bfloat16)
    second_part = contract_last(gate_up_grad, ffn_full)
    ffn_weight_grad = contract_first(second_low, gate_up_grad)
    second_total = lax.psum(second_part, "tp")
    _, second_pull = jax.vjp(rms_norm, resid, second_gain)
    resid_part, second_gain_grad = second_pull(second_total)
    resid_grad = cotangent_full + resid_part
    resid_low = resid_grad.astype(jnp.bfloat16)
    gated_grad = contract_last(resid_low, out_full)
    out_weight_grad = contract_first(gated_low, resid_low)
    _, head_pull = jax.vjp(
        lambda mixed_in, gate_in, gain_in: head_norm(mixed_in, gate_in, gain_in, head_count),
        mixed_flat,
        pre_outgate,
        group_gain,
    )
    mixed_grad, outgate_pre_grad, group_gain_grad = head_pull(gated_grad)
    _, mixer_pull = jax.vjp(
        mixer,
        to_heads(queries),
        to_heads(key_rows),
        to_heads(pre_value),
        to_heads(log_forget),
        state_in,
    )
    first_pass = mixer_pull(
        (to_heads(mixed_grad), jnp.zeros((head_count, HEAD, HEAD), jnp.float32))
    )
    after_pair = carried_in_2((shard_decay, first_pass[4]), "ctx", chain_link, identity)
    second_pass = mixer_pull((jnp.zeros((row_count, head_count, HEAD), jnp.float32), after_pair[1]))
    query_rec_grad = (first_pass[0] + second_pass[0]).reshape(row_count, local_width)
    key_rec_grad = (first_pass[1] + second_pass[1]).reshape(row_count, local_width)
    value_rec_grad = (first_pass[2] + second_pass[2]).reshape(row_count, local_width)
    log_rec_grad = (first_pass[3] + second_pass[3]).reshape(row_count, local_width)
    _, gate_pull = jax.vjp(gate_values, pre_query, pre_forget, forget_bias, bound_vec)
    query_pre_grad, forget_pre_grad, forget_bias_grad, bound_grad = gate_pull(
        (query_rec_grad, key_rec_grad, log_rec_grad)
    )
    _, table_pull = jax.vjp(lambda rows_in: lower_bound(rows_in, layer_index), bound_table)
    (table_grad,) = table_pull(bound_grad)
    proj_grad = jnp.concatenate(
        [query_pre_grad, forget_pre_grad, value_rec_grad, outgate_pre_grad], axis=1
    ).astype(jnp.bfloat16)
    first_part = contract_last(proj_grad, mix_full)
    mix_weight_grad = contract_first(first_low, proj_grad)
    first_total = lax.psum(first_part.astype(jnp.bfloat16), "tp").astype(jnp.float32)
    _, first_pull = jax.vjp(rms_norm, inputs, first_gain)
    input_part, first_gain_grad = first_pull(first_total)
    input_grad = resid_grad + input_part
    mix_summed, out_summed, ffn_summed, down_summed = (
        lax.psum_scatter(
            mix_weight_grad.astype(jnp.bfloat16), ("dp", "ctx"), scatter_dimension=0, tiled=True
        ).astype(jnp.float32),
        lax.psum_scatter(
            out_weight_grad.astype(jnp.bfloat16), ("dp", "ctx"), scatter_dimension=1, tiled=True
        ).astype(jnp.float32),
        lax.psum_scatter(
            ffn_weight_grad.astype(jnp.bfloat16), ("dp", "ctx"), scatter_dimension=0, tiled=True
        ).astype(jnp.float32),
        lax.psum_scatter(
            down_weight_grad.astype(jnp.bfloat16), ("dp", "ctx"), scatter_dimension=1, tiled=True
        ).astype(jnp.float32),
    )
    mix_shard, out_shard, ffn_shard, down_shard = (
        lax.all_gather(mix_summed.astype(jnp.bfloat16), "ctx", axis=0, tiled=True).astype(
            mix_summed.dtype
        ),
        lax.all_gather(out_summed.astype(jnp.bfloat16), "ctx", axis=1, tiled=True).astype(
            out_summed.dtype
        ),
        lax.all_gather(ffn_summed.astype(jnp.bfloat16), "ctx", axis=0, tiled=True).astype(
            ffn_summed.dtype
        ),
        lax.all_gather(down_summed.astype(jnp.bfloat16), "ctx", axis=1, tiled=True).astype(
            down_summed.dtype
        ),
    )
    first_sum, second_sum, group_sum, bias_sum, table_sum = (
        lax.psum(first_gain_grad.astype(jnp.bfloat16), ("dp", "ctx")).astype(jnp.float32),
        lax.psum(second_gain_grad.astype(jnp.bfloat16), ("dp", "ctx")).astype(jnp.float32),
        lax.psum(group_gain_grad.astype(jnp.bfloat16), ("dp", "ctx")).astype(jnp.float32),
        lax.psum(forget_bias_grad.astype(jnp.bfloat16), ("dp", "ctx")).astype(jnp.float32),
        lax.psum(table_grad.astype(jnp.bfloat16), ("dp", "ctx")).astype(jnp.float32),
    )
    return (
        block_out,
        input_grad,
        mix_shard[:, :local_width],
        mix_shard[:, local_width : 2 * local_width],
        mix_shard[:, 2 * local_width : 3 * local_width],
        mix_shard[:, 3 * local_width :],
        out_shard,
        ffn_shard[:, :hidden_width],
        ffn_shard[:, hidden_width:],
        down_shard,
        first_sum,
        second_sum,
        group_sum,
        bias_sum,
        table_sum,
    )


def solution(mesh):
    return jax.shard_map(
        body,
        mesh=mesh,
        in_specs=(
            P(("dp", "ctx"), None),
            P("dp", "tp"),
            P("dp", "tp"),
            P("dp", "tp"),
            P("dp", "tp"),
            P("tp", "dp"),
            P("dp", "tp"),
            P("dp", "tp"),
            P("tp", "dp"),
            P(),
            P(),
            P("tp"),
            P("tp"),
            P(None, "tp"),
            P(),
            P("dp"),
            P(("dp", "ctx"), None),
        ),
        out_specs=(
            P(("dp", "ctx"), None),
            P(("dp", "ctx"), None),
            P("dp", "tp"),
            P("dp", "tp"),
            P("dp", "tp"),
            P("dp", "tp"),
            P("tp", "dp"),
            P("dp", "tp"),
            P("dp", "tp"),
            P("tp", "dp"),
            P(),
            P(),
            P("tp"),
            P("tp"),
            P(None, "tp"),
        ),
        check_vma=False,
    )
```

profile of v0, /device:TPU:0, one launch (start us, length us, event | category | flops | bytes accessed | tf_op | source)
XLA Modules:
  0.0 2218.8 jit_solution(17821822070272523341)
XLA Ops:
  17.0 145.9 %all-gather.8.cloned.1.call-done = bf16[2048,2048]{1,0:T(8,128)(2,1)} async-done(((bf16[512,2048]{1,0:T(8,128)(2,1)}), bf16[2048,2048]{1,0:T(8,128)(2,1)}) %all-gather.8.cloned.1.call-update) | async-done | bytes 8388624 | tf_op jit(solution)/shard_map/all_gather | solution.py:170
  268.4 18.6 pad.557
  312.1 35.5 %pad.734 = f32[31,4,128,128]{2,3,1,0:T(8,128)} pad(f32[16,4,128,128]{2,3,1,0:T(8,128)} %pad_maximum_fusion.5, f32[]{:T(128)} %constant.113.clone.1), padding=0_0_1x0_0_0x0_0_0x0_0_0 | pad | bytes 12320772 | tf_op jit(solution)/shard_map/slice | solution.py:135
  347.6 35.6 %pad.559 = f32[32,4,128,128]{2,3,1,0:T(8,128)} pad(f32[16,4,128,128]{2,3,1,0:T(8,128)} %pad_maximum_fusion.5, f32[]{:T(128)} %constant.113.clone.1), padding=0_1_1x0_0_0x0_0_0x0_0_0 | pad | bytes 12582916 | tf_op jit(solution)/shard_map/pad | solution.py:128
  385.0 35.6 %pad.1005 = f32[32,4,128,128]{2,3,1,0:T(8,128)} pad(f32[16,4,128,128]{2,3,1,0:T(8,128)} %add.591, f32[]{:T(128)} %constant.113.clone.1), padding=1_0_1x0_0_0x0_0_0x0_0_0 | pad | bytes 12582916
  499.8 166.2 %all-reduce.122.cloned.1.call-done = f32[1024,2048]{1,0:T(8,128)} async-done(((f32[1024,2048]{1,0:T(8,128)}), f32[1024,2048]{1,0:T(8,128)}) %all-reduce.122.cloned.1.call-update) | async-done | bytes 8388624 | tf_op jit(solution)/shard_map/psum | solution.py:212
  675.0 194.9 %all-gather.12.cloned.1.call-done = bf16[2048,2816]{1,0:T(8,128)(2,1)} async-done(((bf16[512,2816]{1,0:T(8,128)(2,1)}), bf16[2048,2816]{1,0:T(8,128)(2,1)}) %all-gather.12.cloned.1.call-update) | async-done | bytes 11534352 | tf_op jit(solution)/shard_map/all_gather | solution.py:215
  869.9 20.0 fusion.177
  889.9 86.4 %all-gather.14.cloned.1.call-done = bf16[1408,2048]{1,0:T(8,128)(2,1)} async-done(((bf16[1408,512]{1,0:T(8,128)(2,1)}), bf16[1408,2048]{1,0:T(8,128)(2,1)}) %all-gather.14.cloned.1.call-update) | async-done | bytes 5767184 | tf_op jit(solution)/shard_map/all_gather | solution.py:216
  995.1 16.8 fusion.20
  1054.8 18.7 convolution_convert_fusion
  1084.6 97.8 %all-reduce.124.cloned.1.call-done = f32[1024,2048]{1,0:T(8,128)} async-done(((f32[1024,2048]{1,0:T(8,128)}), f32[1024,2048]{1,0:T(8,128)}) %all-reduce.124.cloned.1.call-update) | async-done | bytes 8388624 | tf_op jit(solution)/shard_map/psum | solution.py:240
  1413.1 18.5 pad.623
  1435.8 18.6 pad.624
  1510.5 35.6 %pad.625 = f32[32,4,128,128]{2,3,1,0:T(8,128)} pad(f32[16,4,128,128]{2,3,1,0:T(8,128)} %get-tuple-element.256, f32[]{:T(128)} %constant.113.clone.1), padding=1_0_1x0_0_0x0_0_0x0_0_0 | pad | bytes 12582916 | tf_op jit(solution)/shard_map/transpose(jvp())/pad | solution.py:128
  1546.0 35.5 %pad.591 = f32[32,4,128,128]{2,3,1,0:T(8,128)} pad(f32[16,4,128,128]{2,3,1,0:T(8,128)} %get-tuple-element.255, f32[]{:T(128)} %constant.113.clone.1), padding=1_0_1x0_0_0x0_0_0x0_0_0 | pad | bytes 12582916 | tf_op jit(solution)/shard_map/transpose(jvp())/pad | solution.py:128
  1590.3 35.6 %pad.592 = f32[32,4,128,128]{2,3,1,0:T(8,128)} pad(f32[16,4,128,128]{2,3,1,0:T(8,128)} %get-tuple-element.375, f32[]{:T(128)} %constant.113.clone.1), padding=0_1_1x0_0_0x0_0_0x0_0_0 | pad | bytes 12582916 | tf_op jit(solution)/shard_map/transpose(jvp())/pad | solution.py:128
  1625.9 35.7 %pad.626 = f32[32,4,128,128]{2,3,1,0:T(8,128)} pad(f32[16,4,128,128]{2,3,1,0:T(8,128)} %get-tuple-element.376, f32[]{:T(128)} %constant.113.clone.1), padding=0_1_1x0_0_0x0_0_0x0_0_0 | pad | bytes 12582916 | tf_op jit(solution)/shard_map/transpose(jvp())/pad | solution.py:128
  1661.7 33.6 %pad.562 = f32[32,4,128,128]{2,3,1,0:T(8,128)} pad(f32[15,4,128,128]{2,3,1,0:T(8,128)} %get-tuple-element.290, f32[]{:T(128)} %constant.113.clone.1), padding=2_1_1x0_0_0x0_0_0x0_0_0 | pad | bytes 12320772 | tf_op jit(solution)/shard_map/transpose(jvp())/pad | solution.py:128
  1695.3 33.7 %pad.597 = f32[32,4,128,128]{2,3,1,0:T(8,128)} pad(f32[15,4,128,128]{2,3,1,0:T(8,128)} %get-tuple-element.291, f32[]{:T(128)} %constant.113.clone.1), padding=2_1_1x0_0_0x0_0_0x0_0_0 | pad | bytes 12320772 | tf_op jit(solution)/shard_map/transpose(jvp())/pad | solution.py:128
  1810.3 19.3 fusion.176
  1913.4 152.0 %all-reduce.126.cloned.1.call-done = (bf16[1024,2048]{1,0:T(8,128)(2,1)}, bf16[1024,2048]{1,0:T(8,128)(2,1)}) async-done(((bf16[1024,2048]{1,0:T(8,128)(2,1)}, bf16[1024,2048]{1,0:T(8,128)(2,1)}), (bf16[1024,2048]{1,0:T(8,128)(2,1)}, bf16[1024,2048]{1,0:T(8,128)(2,1)})) %all-reduce.126.cloned.1.call-update) | async-done | bytes 8388624 | tf_op jit(solution)/shard_map/psum | solution.py:224
  2073.8 84.8 %reduce-scatter.5.cloned.1.call-done = bf16[256,2048]{1,0:T(8,128)(2,1)} async-done(((bf16[2048,2048]{1,0:T(8,128)(2,1)}), bf16[256,2048]{1,0:T(8,128)(2,1)}) %reduce-scatter.5.cloned.1.call-update) | async-done | bytes 1048592 | tf_op jit(solution)/shard_map/reduce_scatter | solution.py:287
  2164.6 26.3 %all-reduce.116 = (bf16[2048]{0:T(1024)(128)(2,1)S(1)}, bf16[2048]{0:T(1024)(128)(2,1)S(1)}, bf16[512]{0:T(512)(128)(2,1)S(1)}, bf16[512]{0:T(512)(128)(2,1)S(1)}, bf16[24,512]{1,0:T(8,128)(2,1)S(1)}) all-reduce(bf16[2048]{0:T(1024)(128)(2,1)S(1)} %get-tuple-element.200, ...), channel_id=1, replica_groups=mesh['dp'=4,'ctx'=2,'tp'=4] {'dp','ctx'}, use_global_device_ids=true, to_apply=%region_51.52 | all-reduce | flops 17408 | bytes 69632 | tf_op jit(solution)/shard_map/psum | solution.py:315
  (832 shorter events, 799.1 us)
Async XLA Ops:
  7.2 155.7 %all-gather.8.cloned.1.call-start = ((), (), s32[]{:S(2)}) async-start(), calls=%async_computation.4 | async-start | bytes 10485760 | tf_op jit(solution)/shard_map/all_gather | solution.py:170
  10.4 477.5 %all-gather.10.cloned.1.call-start = ((), (), s32[]{:S(2)}) async-start(), calls=%async_computation.5 | async-start | bytes 2621440 | tf_op jit(solution)/shard_map/all_gather | solution.py:171
  11.1 654.9 %all-reduce.122.cloned.1.call-start = ((), (), s32[]{:S(2)}) async-start(), calls=%async_computation.6 | async-start | bytes 16777216 | tf_op jit(solution)/shard_map/psum | solution.py:212
  16.4 159.0 %copy-start.171 = (f32[1024]{0:T(1024)}, f32[1024]{0:T(1024)S(1)}, u32[]{:S(2)}) copy-start(f32[1024]{0:T(1024)S(1)} %fusion.149) | copy-start | bytes 12292
  16.6 158.8 %copy-start.178 = (f32[512]{0:T(512)}, f32[512]{0:T(512)S(1)}, u32[]{:S(2)}) copy-start(f32[512]{0:T(512)S(1)} %multiply_reduce_fusion.28) | copy-start | bytes 6148
  16.6 158.8 %copy-start.196 = (f32[512]{0:T(512)}, f32[512]{0:T(512)S(1)}, u32[]{:S(2)}) copy-start(f32[512]{0:T(512)S(1)} %broadcast_subtract_fusion) | copy-start | bytes 6148
  16.7 169.4 %copy-start.214 = (f32[32]{0:T(128)}, f32[32]{0:T(128)S(1)}, u32[]{:S(2)}) copy-start(f32[32]{0:T(128)S(1)} %get-tuple-element.269) | copy-start | bytes 388
  16.9 1024.1 %copy-start.73 = (pred[32,32,32]{2,1,0:T(8,128)(4,1)}, pred[32,32,32]{2,1,0:T(8,128)(4,1)S(1)}, u32[]{:S(2)}) copy-start(pred[32,32,32]{2,1,0:T(8,128)(4,1)S(1)} %compare_and_fusion) | copy-start | bytes 98308
  16.9 189.3 %copy-start.131 = (f32[32,32]{0,1:T(8,128)}, f32[32,32]{0,1:T(8,128)S(1)}, u32[]{:S(2)}) copy-start(f32[32,32]{0,1:T(8,128)S(1)} %get-tuple-element.440) | copy-start | bytes 12292
  16.9 415.8 %copy-start.129 = (f32[32,32]{0,1:T(8,128)}, f32[32,32]{0,1:T(8,128)S(1)}, u32[]{:S(2)}) copy-start(f32[32,32]{0,1:T(8,128)S(1)} %get-tuple-element.439) | copy-start | bytes 12292
  17.0 158.5 %copy-start.204 = (f32[512]{0:T(512)S(1)}, f32[512]{0:T(512)}, u32[]{:S(2)}) copy-start(f32[512]{0:T(512)} %param.31) | copy-start | bytes 6148
  424.2 600.7 %copy-start.88 = (f32[1,4,128,128]{2,3,1,0:T(8,128)}, f32[1,4,128,128]{2,3,1,0:T(8,128)S(1)}, u32[]{:S(2)}) copy-start(f32[1,4,128,128]{2,3,1,0:T(8,128)S(1)} %add_select_fusion) | copy-start | bytes 786436
  495.5 374.3 %all-gather.12.cloned.1.call-start = ((), (), s32[]{:S(2)}) async-start(), calls=%async_computation.7 | async-start | bytes 14417920 | tf_op jit(solution)/shard_map/all_gather | solution.py:215
  499.2 477.1 %all-gather.14.cloned.1.call-start = ((), (), s32[]{:S(2)}) async-start(), calls=%async_computation.8 | async-start | bytes 7208960 | tf_op jit(solution)/shard_map/all_gather | solution.py:216
  499.7 370.1 %copy-start.177 = (f32[2048]{0:T(1024)S(1)}, f32[2048]{0:T(1024)}, u32[]{:S(2)}) copy-start(f32[2048]{0:T(1024)} %param.29) | copy-start | bytes 24580
  499.8 682.7 %all-reduce.124.cloned.1.call-start = ((), (), s32[]{:S(2)}) async-start(), calls=%async_computation.9 | async-start | bytes 16777216 | tf_op jit(solution)/shard_map/psum | solution.py:240
  1011.9 865.1 %reduce-scatter.11.cloned.1.call-start = ((), (), s32[]{:S(2)}) async-start(), calls=%async_computation.15 | async-start | bytes 6488064 | tf_op jit(solution)/shard_map/reduce_scatter | solution.py:296
  1022.5 882.9 %reduce-scatter.9.cloned.1.call-start = ((), (), s32[]{:S(2)}) async-start(), calls=%async_computation.13 | async-start | bytes 12976128 | tf_op jit(solution)/shard_map/reduce_scatter | solution.py:293
  1073.5 833.1 %reduce-scatter.7.cloned.1.call-start = ((), (), s32[]{:S(2)}) async-start(), calls=%async_computation.12 | async-start | bytes 2359296 | tf_op jit(solution)/shard_map/reduce_scatter | solution.py:290
  1808.8 101.3 %all-gather.20.cloned.1.call-start = ((), (), s32[]{:S(2)}) async-start(), calls=%async_computation.16 | async-start | bytes 2162688 | tf_op jit(solution)/shard_map/all_gather | solution.py:310
  1877.1 188.4 %all-reduce.126.cloned.1.call-start = ((), (), s32[]{:S(2)}) async-start(), calls=%async_computation.17 | async-start | bytes 16777216 | tf_op jit(solution)/shard_map/psum | solution.py:224
  1890.0 268.6 %reduce-scatter.5.cloned.1.call-start = ((), (), s32[]{:S(2)}) async-start(), calls=%async_computation.10 | async-start | bytes 9437184 | tf_op jit(solution)/shard_map/reduce_scatter | solution.py:287
  1905.3 298.1 %all-gather.18.cloned.1.call-start = ((), (), s32[]{:S(2)}) async-start(), calls=%async_computation.14 | async-start | bytes 4325376 | tf_op jit(solution)/shard_map/all_gather | solution.py:307
  1906.0 302.0 %all-gather.16.cloned.1.call-start = ((), (), s32[]{:S(2)}) async-start(), calls=%async_computation.11 | async-start | bytes 3145728 | tf_op jit(solution)/shard_map/all_gather | solution.py:301
  (237 other events, 2089.7 us)
Sparse Core Ops, SparseCore 0:
  10.5 152.3 all-gather.7
  164.4 44.1 all-gather.9
  495.6 170.3 all-reduce.121
  668.1 201.7 all-gather.11
  871.3 104.8 all-gather.13
  1012.0 170.3 all-reduce.123
  1184.7 65.5 reduce-scatter.10
  1252.6 117.6 reduce-scatter.8
  1808.8 36.2 reduce-scatter.6
  1877.2 10.0 all-gather.19
  1891.6 173.7 all-reduce.125
  2068.3 90.2 reduce-scatter.4
  2160.2 10.1 all-gather.17
  2171.8 11.7 all-gather.15
where the time goes:
time: 2250 us; the launch traced here: 2220 us
  waiting for transfers between devices  930 us (41%)
  local copies, waits for them, and re-layouts  640 us (28%)
  matrix products  319 us (14%)
  other arithmetic  275 us (12%)
  blocking collectives  36.4 us (2%)
    pad x74, local copies, waits for them, and re-layouts, block_parts(): lax.associative_scan(chain_link, (carried, states), axis=0)  483 us
    all_gather x1, waiting for transfers between devices, body(): lax.all_gather(ffn_local, 'dp', axis=0, tiled=True)  195 us
    psum x1, waiting for transfers between devices, body(): resid = inputs + lax.psum(mix_partial, 'tp')  166 us
    psum x1, waiting for transfers between devices, body(): lax.psum(ffn_partial.astype(jnp.bfloat16), 'tp').astype(jnp.float32)  152 us
    all_gather x1, waiting for transfers between devices, body(): lax.all_gather(mix_local, 'dp', axis=0, tiled=True)  146 us
    psum x1, waiting for transfers between devices, body(): second_total = lax.psum(second_part, 'tp')  97.8 us
    all_gather x1, waiting for transfers between devices, body(): lax.all_gather(ffn_down, 'dp', axis=1, tiled=True)  86.4 us
    reduce_scatter x1, waiting for transfers between devices, body(): lax.psum_scatter(mix_weight_grad.astype(jnp.bfloat16), ('dp', 'ctx'), sca...  84.8 us
  transfers between devices with their start and end apart: 14, of which 7 were waited for; matrix products, arithmetic and copies ran while one was open for 51% of the time, Pallas kernels for 0%

commit v1 on v0

--- a/solution.py
+++ b/solution.py
@@ -8,6 +8,24 @@
 HIGH = lax.Precision.HIGHEST
 EPS_NORM = 1e-06
 EPS_GROUP = 1e-05
+
+
+def manage_the_sheets(block_here, chip_axis):
+    state_now = lax.axis_size(chip_axis)
+    local_out = lax.axis_index(chip_axis)
+    newest, view_out, plain = (state_now, local_out, block_here.shape[0])
+    parts_seen = [w * newest if c == 0 else w for c, w in enumerate(block_here.shape)]
+    lower = lax.dynamic_update_slice_in_dim(
+        jnp.zeros(parts_seen, block_here.dtype), block_here, view_out * plain, axis=0
+    )
+    for dev_i in range(1, newest):
+        block_here = lax.ppermute(
+            block_here, chip_axis, [(c, (c + 1) % newest) for c in range(newest)]
+        )
+        lower = lax.dynamic_update_slice_in_dim(
+            lower, block_here, (view_out - dev_i) % newest * plain, axis=0
+        )
+    return lower
 
 
 def carried_in(value, axis, join, neutral):
@@ -212,7 +230,7 @@
     resid = inputs + lax.psum(mix_partial, "tp")
     second_low = rms_norm(resid, second_gain).astype(jnp.bfloat16)
     ffn_full, down_full = (
-        lax.all_gather(ffn_local, "dp", axis=0, tiled=True),
+        manage_the_sheets(ffn_local, "dp"),
         lax.all_gather(ffn_down, "dp", axis=1, tiled=True),
     )
     gate_up = jnp.dot(second_low, ffn_full, preferred_element_type=jnp.float32)

time: 2250 us -> 2250 us (level)
  local copies, waits for them, and re-layouts: 640 us -> 665 us
    ppermute x0 -> x3, waiting for transfers between devices: none -> 200 us  [manage_the_sheets(): lax.ppermute(block_here, chip_axis, [(c, (c + 1) % newest) for c in range...]
    psum x1, waiting for transfers between devices: 166 us -> 0.01 us  [body(): resid = inputs + lax.psum(mix_partial, 'tp')]
    all_gather x1, waiting for transfers between devices: 86.4 us -> 44.6 us  [body(): lax.all_gather(ffn_down, 'dp', axis=1, tiled=True)]
    unnamed x468 -> x469, local copies, waits for them, and re-layouts: 79.2 us -> 82.4 us
  transfers between devices with their start and end apart: 14 -> 17, of which waited for: 7 -> 9; matrix products, arithmetic and copies ran while one was open for 51% -> 53% of each run, Pallas kernels for 0% -> 0%
where the time goes in v1:
time: 2250 us; the launch traced here: 2220 us
  waiting for transfers between devices  911 us (40%)
  local copies, waits for them, and re-layouts  665 us (30%)
  matrix products  319 us (14%)
  other arithmetic  267 us (12%)
  blocking collectives  36.4 us (2%)
    pad x74, local copies, waits for them, and re-layouts, block_parts(): lax.associative_scan(chain_link, (carried, states), axis=0)  484 us
    ppermute x3, waiting for transfers between devices, manage_the_sheets(): lax.ppermute(block_here, chip_axis, [(c, (c + 1) % newest) for c in range...  200 us
    all_gather x1, waiting for transfers between devices, body(): lax.all_gather(ffn_local, 'dp', axis=0, tiled=True)  184 us
    psum x1, waiting for transfers between devices, body(): lax.psum(ffn_partial.astype(jnp.bfloat16), 'tp').astype(jnp.float32)  152 us
    all_gather x1, waiting for transfers between devices, body(): lax.all_gather(mix_local, 'dp', axis=0, tiled=True)  146 us
    psum x1, waiting for transfers between devices, body(): second_total = lax.psum(second_part, 'tp')  97.7 us
    reduce_scatter x1, waiting for transfers between devices, body(): lax.psum_scatter(mix_weight_grad.astype(jnp.bfloat16), ('dp', 'ctx'), sca...  84.9 us
    unnamed x469, local copies, waits for them, and re-layouts  82.4 us
  transfers between devices with their start and end apart: 17, of which 9 were waited for; matrix products, arithmetic and copies ran while one was open for 53% of the time, Pallas kernels for 0%

profile of v1, /device:TPU:0, one launch (start us, length us, event | category | flops | bytes accessed | tf_op | source)
XLA Modules:
  0.0 2218.3 jit_solution(7412519946979133656)
XLA Ops:
  17.0 145.9 %all-gather.8.cloned.1.call-done = bf16[2048,2048]{1,0:T(8,128)(2,1)} async-done(((bf16[512,2048]{1,0:T(8,128)(2,1)}), bf16[2048,2048]{1,0:T(8,128)(2,1)}) %all-gather.8.cloned.1.call-update) | async-done | bytes 8388624 | tf_op jit(solution)/shard_map/all_gather | solution.py:188
  268.4 18.7 pad.557
  312.0 35.6 %pad.732 = f32[31,4,128,128]{2,3,1,0:T(8,128)} pad(f32[16,4,128,128]{2,3,1,0:T(8,128)} %pad_maximum_fusion.5, f32[]{:T(128)} %constant.142.clone.1), padding=0_0_1x0_0_0x0_0_0x0_0_0 | pad | bytes 12320772 | tf_op jit(solution)/shard_map/slice | solution.py:153
  347.6 35.4 %pad.559 = f32[32,4,128,128]{2,3,1,0:T(8,128)} pad(f32[16,4,128,128]{2,3,1,0:T(8,128)} %pad_maximum_fusion.5, f32[]{:T(128)} %constant.142.clone.1), padding=0_1_1x0_0_0x0_0_0x0_0_0 | pad | bytes 12582916 | tf_op jit(solution)/shard_map/pad | solution.py:146
  384.8 35.5 %pad.1001 = f32[32,4,128,128]{2,3,1,0:T(8,128)} pad(f32[16,4,128,128]{2,3,1,0:T(8,128)} %add.616, f32[]{:T(128)} %constant.142.clone.1), padding=1_0_1x0_0_0x0_0_0x0_0_0 | pad | bytes 12582916
  499.3 66.6 %collective-permute-done = bf16[512,2816]{1,0:T(8,128)(2,1)} collective-permute-done((bf16[512,2816]{1,0:T(8,128)(2,1)}, bf16[512,2816]{1,0:T(8,128)(2,1)}, u32[]{:S(2)}, u32[]{:S(2)}) %collective-permute-start) | collective-permute-done | bytes 2883616 | tf_op jit(solution)/shard_map/ppermute | solution.py:22
  565.9 65.9 %collective-permute-done.1 = bf16[512,2816]{1,0:T(8,128)(2,1)} collective-permute-done((bf16[512,2816]{1,0:T(8,128)(2,1)}, bf16[512,2816]{1,0:T(8,128)(2,1)}, u32[]{:S(2)}, u32[]{:S(2)}) %collective-permute-start.1) | collective-permute-done | bytes 2883616 | tf_op jit(solution)/shard_map/ppermute | solution.py:22
  648.1 67.1 %collective-permute-done.2 = bf16[512,2816]{1,0:T(8,128)(2,1)} collective-permute-done((bf16[512,2816]{1,0:T(8,128)(2,1)}, bf16[512,2816]{1,0:T(8,128)(2,1)}, u32[]{:S(2)}, u32[]{:S(2)}) %collective-permute-start.2) | collective-permute-done | bytes 2883616 | tf_op jit(solution)/shard_map/ppermute | solution.py:22
  745.5 44.6 %all-gather.12.cloned.1.call-done = bf16[1408,2048]{1,0:T(8,128)(2,1)} async-done(((bf16[1408,512]{1,0:T(8,128)(2,1)}), bf16[1408,2048]{1,0:T(8,128)(2,1)}) %all-gather.12.cloned.1.call-update) | async-done | bytes 5767184 | tf_op jit(solution)/shard_map/all_gather | solution.py:234
  807.3 184.2 %all-gather.14.cloned.1.call-done = bf16[2048,2816]{1,0:T(8,128)(2,1)} async-done(((bf16[512,2816]{1,0:T(8,128)(2,1)}), bf16[2048,2816]{1,0:T(8,128)(2,1)}) %all-gather.14.cloned.1.call-update) | async-done | bytes 11534352 | tf_op jit(solution)/shard_map/all_gather | solution.py:247
  991.5 18.7 fusion.20
  1053.2 18.6 convolution_convert_fusion
  1082.9 97.7 %all-reduce.124.cloned.1.call-done = f32[1024,2048]{1,0:T(8,128)} async-done(((f32[1024,2048]{1,0:T(8,128)}), f32[1024,2048]{1,0:T(8,128)}) %all-reduce.124.cloned.1.call-update) | async-done | bytes 8388624 | tf_op jit(solution)/shard_map/psum | solution.py:258
  1434.2 18.7 pad.624
  1509.2 35.6 %pad.625 = f32[32,4,128,128]{2,3,1,0:T(8,128)} pad(f32[16,4,128,128]{2,3,1,0:T(8,128)} %get-tuple-element.256, f32[]{:T(128)} %constant.142.clone.1), padding=1_0_1x0_0_0x0_0_0x0_0_0 | pad | bytes 12582916 | tf_op jit(solution)/shard_map/transpose(jvp())/pad | solution.py:146
  1544.8 35.8 %pad.591 = f32[32,4,128,128]{2,3,1,0:T(8,128)} pad(f32[16,4,128,128]{2,3,1,0:T(8,128)} %get-tuple-element.255, f32[]{:T(128)} %constant.142.clone.1), padding=1_0_1x0_0_0x0_0_0x0_0_0 | pad | bytes 12582916 | tf_op jit(solution)/shard_map/transpose(jvp())/pad | solution.py:146
  1589.4 35.7 %pad.592 = f32[32,4,128,128]{2,3,1,0:T(8,128)} pad(f32[16,4,128,128]{2,3,1,0:T(8,128)} %get-tuple-element.375, f32[]{:T(128)} %constant.142.clone.1), padding=0_1_1x0_0_0x0_0_0x0_0_0 | pad | bytes 12582916 | tf_op jit(solution)/shard_map/transpose(jvp())/pad | solution.py:146
  1625.1 35.7 %pad.626 = f32[32,4,128,128]{2,3,1,0:T(8,128)} pad(f32[16,4,128,128]{2,3,1,0:T(8,128)} %get-tuple-element.376, f32[]{:T(128)} %constant.142.clone.1), padding=0_1_1x0_0_0x0_0_0x0_0_0 | pad | bytes 12582916 | tf_op jit(solution)/shard_map/transpose(jvp())/pad | solution.py:146
  1660.9 33.6 %pad.562 = f32[32,4,128,128]{2,3,1,0:T(8,128)} pad(f32[15,4,128,128]{2,3,1,0:T(8,128)} %get-tuple-element.290, f32[]{:T(128)} %constant.142.clone.1), padding=2_1_1x0_0_0x0_0_0x0_0_0 | pad | bytes 12320772 | tf_op jit(solution)/shard_map/transpose(jvp())/pad | solution.py:146
  1694.5 33.8 %pad.597 = f32[32,4,128,128]{2,3,1,0:T(8,128)} pad(f32[15,4,128,128]{2,3,1,0:T(8,128)} %get-tuple-element.291, f32[]{:T(128)} %constant.142.clone.1), padding=2_1_1x0_0_0x0_0_0x0_0_0 | pad | bytes 12320772 | tf_op jit(solution)/shard_map/transpose(jvp())/pad | solution.py:146
  1809.7 19.4 fusion.176
  1912.8 152.1 %all-reduce.126.cloned.1.call-done = (bf16[1024,2048]{1,0:T(8,128)(2,1)}, bf16[1024,2048]{1,0:T(8,128)(2,1)}) async-done(((bf16[1024,2048]{1,0:T(8,128)(2,1)}, bf16[1024,2048]{1,0:T(8,128)(2,1)}), (bf16[1024,2048]{1,0:T(8,128)(2,1)}, bf16[1024,2048]{1,0:T(8,128)(2,1)})) %all-reduce.126.cloned.1.call-update) | async-done | bytes 8388624 | tf_op jit(solution)/shard_map/psum | solution.py:242
  2073.2 84.9 %reduce-scatter.5.cloned.1.call-done = bf16[256,2048]{1,0:T(8,128)(2,1)} async-done(((bf16[2048,2048]{1,0:T(8,128)(2,1)}), bf16[256,2048]{1,0:T(8,128)(2,1)}) %reduce-scatter.5.cloned.1.call-update) | async-done | bytes 1048592 | tf_op jit(solution)/shard_map/reduce_scatter | solution.py:305
  2164.1 26.3 %all-reduce.116 = (bf16[2048]{0:T(1024)(128)(2,1)S(1)}, bf16[2048]{0:T(1024)(128)(2,1)S(1)}, bf16[512]{0:T(512)(128)(2,1)S(1)}, bf16[512]{0:T(512)(128)(2,1)S(1)}, bf16[24,512]{1,0:T(8,128)(2,1)S(1)}) all-reduce(bf16[2048]{0:T(1024)(128)(2,1)S(1)} %get-tuple-element.200, ...), channel_id=1, replica_groups=mesh['dp'=4,'ctx'=2,'tp'=4] {'dp','ctx'}, use_global_device_ids=true, to_apply=%region_51.52 | all-reduce | flops 17408 | bytes 69632 | tf_op jit(solution)/shard_map/psum | solution.py:333
  (844 shorter events, 853.7 us)
Async XLA Ops:
  7.2 155.7 %all-gather.8.cloned.1.call-start = ((), (), s32[]{:S(2)}) async-start(), calls=%async_computation.4 | async-start | bytes 10485760 | tf_op jit(solution)/shard_map/all_gather | solution.py:188
  10.4 476.8 %all-gather.10.cloned.1.call-start = ((), (), s32[]{:S(2)}) async-start(), calls=%async_computation.5 | async-start | bytes 2621440 | tf_op jit(solution)/shard_map/all_gather | solution.py:189
  11.1 707.8 %all-reduce.122.cloned.1.call-start = ((), (), s32[]{:S(2)}) async-start(), calls=%async_computation.6 | async-start | bytes 16777216 | tf_op jit(solution)/shard_map/psum | solution.py:230
  16.4 159.0 %copy-start.173 = (f32[1024]{0:T(1024)}, f32[1024]{0:T(1024)S(1)}, u32[]{:S(2)}) copy-start(f32[1024]{0:T(1024)S(1)} %fusion.149) | copy-start | bytes 12292
  16.6 158.8 %copy-start.198 = (f32[512]{0:T(512)}, f32[512]{0:T(512)S(1)}, u32[]{:S(2)}) copy-start(f32[512]{0:T(512)S(1)} %broadcast_subtract_fusion) | copy-start | bytes 6148
  16.7 169.3 %copy-start.216 = (f32[32]{0:T(128)}, f32[32]{0:T(128)S(1)}, u32[]{:S(2)}) copy-start(f32[32]{0:T(128)S(1)} %get-tuple-element.269) | copy-start | bytes 388
  16.9 1022.5 %copy-start.74 = (pred[32,32,32]{2,1,0:T(8,128)(4,1)}, pred[32,32,32]{2,1,0:T(8,128)(4,1)S(1)}, u32[]{:S(2)}) copy-start(pred[32,32,32]{2,1,0:T(8,128)(4,1)S(1)} %compare_and_fusion) | copy-start | bytes 98308
  16.9 189.2 %copy-start.133 = (f32[32,32]{0,1:T(8,128)}, f32[32,32]{0,1:T(8,128)S(1)}, u32[]{:S(2)}) copy-start(f32[32,32]{0,1:T(8,128)S(1)} %get-tuple-element.440) | copy-start | bytes 12292
  16.9 415.5 %copy-start.131 = (f32[32,32]{0,1:T(8,128)}, f32[32,32]{0,1:T(8,128)S(1)}, u32[]{:S(2)}) copy-start(f32[32,32]{0,1:T(8,128)S(1)} %get-tuple-element.439) | copy-start | bytes 12292
  423.9 599.3 %copy-start.89 = (f32[1,4,128,128]{2,3,1,0:T(8,128)}, f32[1,4,128,128]{2,3,1,0:T(8,128)S(1)}, u32[]{:S(2)}) copy-start(f32[1,4,128,128]{2,3,1,0:T(8,128)S(1)} %add_select_fusion) | copy-start | bytes 786436
  494.7 295.4 %all-gather.12.cloned.1.call-start = ((), (), s32[]{:S(2)}) async-start(), calls=%async_computation.7 | async-start | bytes 7208960 | tf_op jit(solution)/shard_map/all_gather | solution.py:234
  495.3 496.3 %all-gather.14.cloned.1.call-start = ((), (), s32[]{:S(2)}) async-start(), calls=%async_computation.8 | async-start | bytes 14417920 | tf_op jit(solution)/shard_map/all_gather | solution.py:247
  499.2 66.7 %collective-permute-start = (bf16[512,2816]{1,0:T(8,128)(2,1)}, bf16[512,2816]{1,0:T(8,128)(2,1)}, u32[]{:S(2)}, u32[]{:S(2)}) collective-permute-start(bf16[512,2816]{1,0:T(8,128)(2,1)} %constant_dynamic-update-slice_fusion), channel_id=1, source_target_pairs={{0,8},{8,16},{16,24},{24,0},{1,9},{9,17},{17,25},{25,1},{2,10},{10... | collective-permute-start | bytes 8650760 | tf_op jit(solution)/shard_map/ppermute | solution.py:22
  499.2 681.4 %all-reduce.124.cloned.1.call-start = ((), (), s32[]{:S(2)}) async-start(), calls=%async_computation.9 | async-start | bytes 16777216 | tf_op jit(solution)/shard_map/psum | solution.py:258
  565.9 65.9 %collective-permute-start.1 = (bf16[512,2816]{1,0:T(8,128)(2,1)}, bf16[512,2816]{1,0:T(8,128)(2,1)}, u32[]{:S(2)}, u32[]{:S(2)}) collective-permute-start(bf16[512,2816]{1,0:T(8,128)(2,1)} %collective-permute-done), channel_id=1, source_target_pairs={{0,8},{8,16},{16,24},{24,0},{1,9},{9,17},{17,25},{25,1},{2,10},{10... | collective-permute-start | bytes 8650760 | tf_op jit(solution)/shard_map/ppermute | solution.py:22
  631.8 83.5 %collective-permute-start.2 = (bf16[512,2816]{1,0:T(8,128)(2,1)}, bf16[512,2816]{1,0:T(8,128)(2,1)}, u32[]{:S(2)}, u32[]{:S(2)}) collective-permute-start(bf16[512,2816]{1,0:T(8,128)(2,1)} %collective-permute-done.1), channel_id=1, source_target_pairs={{0,8},{8,16},{16,24},{24,0},{1,9},{9,17},{17,25},{25,1},{2,10},{10... | collective-permute-start | bytes 8650760 | tf_op jit(solution)/shard_map/ppermute | solution.py:22
  1010.2 866.2 %reduce-scatter.11.cloned.1.call-start = ((), (), s32[]{:S(2)}) async-start(), calls=%async_computation.15 | async-start | bytes 6488064 | tf_op jit(solution)/shard_map/reduce_scatter | solution.py:314
  1020.8 884.0 %reduce-scatter.9.cloned.1.call-start = ((), (), s32[]{:S(2)}) async-start(), calls=%async_computation.13 | async-start | bytes 12976128 | tf_op jit(solution)/shard_map/reduce_scatter | solution.py:311
  1071.8 834.2 %reduce-scatter.7.cloned.1.call-start = ((), (), s32[]{:S(2)}) async-start(), calls=%async_computation.12 | async-start | bytes 2359296 | tf_op jit(solution)/shard_map/reduce_scatter | solution.py:308
  1808.1 101.4 %all-gather.20.cloned.1.call-start = ((), (), s32[]{:S(2)}) async-start(), calls=%async_computation.16 | async-start | bytes 2162688 | tf_op jit(solution)/shard_map/all_gather | solution.py:328
  1876.5 188.4 %all-reduce.126.cloned.1.call-start = ((), (), s32[]{:S(2)}) async-start(), calls=%async_computation.17 | async-start | bytes 16777216 | tf_op jit(solution)/shard_map/psum | solution.py:242
  1889.5 268.6 %reduce-scatter.5.cloned.1.call-start = ((), (), s32[]{:S(2)}) async-start(), calls=%async_computation.10 | async-start | bytes 9437184 | tf_op jit(solution)/shard_map/reduce_scatter | solution.py:305
  1904.7 298.2 %all-gather.18.cloned.1.call-start = ((), (), s32[]{:S(2)}) async-start(), calls=%async_computation.14 | async-start | bytes 4325376 | tf_op jit(solution)/shard_map/all_gather | solution.py:325
  1905.5 302.1 %all-gather.16.cloned.1.call-start = ((), (), s32[]{:S(2)}) async-start(), calls=%async_computation.11 | async-start | bytes 3145728 | tf_op jit(solution)/shard_map/all_gather | solution.py:319
  (240 other events, 2420.4 us)
Sparse Core Ops, SparseCore 0:
  10.5 152.3 all-gather.7
  164.4 44.1 all-gather.9
  494.8 170.3 all-reduce.121
  666.7 123.4 all-gather.11
  792.2 199.2 all-gather.13
  1010.4 170.2 all-reduce.123
  1183.0 65.5 reduce-scatter.10
  1250.9 117.6 reduce-scatter.8
  1808.1 36.3 reduce-scatter.6
  1876.6 10.0 all-gather.19
  1891.1 173.7 all-reduce.125
  2067.8 90.2 reduce-scatter.4
  2159.7 10.1 all-gather.17
  2171.3 11.7 all-gather.15
